TPU v7x, 32 devices: a whole 2x2x4 slice. The times are simulated.
32 devices in a mesh: section: 2 (over y), dp: 16 (over z, x, core).
Axes of the slice: x: 2, y: 2, z: 4, core: 2. Of those that a mesh axis runs over, the one named last changes fastest.
Arguments:
- tokens: bfloat16 [2, 4096, 768], P(None, 'dp'), may hold values from -6 to 6
- lengths: int32 [2, 16], replicated, may hold values from 200 to 256
- w_qkv: float32 [2, 768, 2304], P('section', 'dp'), may hold values from -0.21875 to 0.21875
- w_out: float32 [2, 768, 768], P('section', 'dp'), may hold values from -0.625 to 0.625
- w_gate_up: float32 [2, 768, 6144], P('section', 'dp'), may hold values from -0.21875 to 0.21875
- w_down: float32 [2, 3072, 768], P('section', 'dp'), may hold values from -0.109375 to 0.109375
- norm_gain: float32 [2, 2, 768], P('section', None, 'dp'), may hold values from 0.25 to 1.75
- norm_bias: float32 [2, 2, 768], P('section', None, 'dp'), may hold values from -3 to 3
- cotangent: bfloat16 [2, 4096, 768], P(None, 'dp'), may hold values from -6 to 6
Outputs:
- layer_outputs: bfloat16 [2, 2, 4096, 768], P('section', None, 'dp')
- input_grads: float32 [2, 2, 4096, 768], P('section', None, 'dp')
- grad_w_qkv: float32 [2, 768, 2304], P('section', 'dp')
- grad_w_out: float32 [2, 768, 768], P('section', 'dp')
- grad_w_gate_up: float32 [2, 768, 6144], P('section', 'dp')
- grad_w_down: float32 [2, 3072, 768], P('section', 'dp')
- grad_norm_gain: float32 [2, 2, 768], P('section', None, 'dp')
- grad_norm_bias: float32 [2, 2, 768], P('section', None, 'dp')
Inputs may be any that keep to these rules, and one draw needn't show every extreme that they name: `lengths`: positions of a window from its length on are padding.
All inputs are finite; a program needn't handle non-finite values.
Results may differ from a plain program's by a relative error of at most 0.024.
The roundings to bfloat16 on the way count: a program that leaves them out, or rounds other values in their place, can miss the bound.
Values may be sent and summed in bfloat16 or wider, within the bound.
No kernel may reach another device: no remote copies, remote signals or barrier semaphores. Data moves between devices by JAX's collectives and lax.ppermute only.
A program may use at most 256 MiB of HBM per device.

v0:
```python
import jax
import jax.numpy as jnp
from jax import lax
from jax.sharding import PartitionSpec as P

D = 768
HEADS = 12
HEAD = 64
FF = 3072
EPSILON = 1e-05
NEGATIVE = -1e30


def shifted(shard, axis, by):
    devices = lax.axis_size(axis)
    pairs = [(i, i + by) for i in range(devices) if 0 <= i + by < devices]
    return lax.ppermute(shard, axis, pairs)


def norm_forward(row_values, gain_row, bias_row):
    center = row_values - jnp.mean(row_values, axis=-1, keepdims=True)
    scale_inv = lax.rsqrt(jnp.mean(center * center, axis=-1, keepdims=True) + EPSILON)
    normed = center * scale_inv
    return (normed * gain_row + bias_row, normed, scale_inv)


def norm_backward(upstream, normed, scale_inv, gain_row):
    scaled = upstream * gain_row
    inner_sum = (
        scaled
        - jnp.mean(scaled, axis=-1, keepdims=True)
        - normed * jnp.mean(scaled * normed, axis=-1, keepdims=True)
    )
    return (scale_inv * inner_sum, jnp.sum(upstream * normed, axis=0), jnp.sum(upstream, axis=0))


def score_block(queries, keys_all, length):
    seq_rows = queries.shape[0]
    slopes = jnp.exp2(-8.0 * (jnp.arange(HEADS).astype(jnp.float32) + 1.0) / HEADS)
    raw_scores = jnp.einsum(
        "qhd,khd->hqk", queries, keys_all, preferred_element_type=jnp.float32
    ) * HEAD ** (-0.5)
    places = jnp.arange(seq_rows, dtype=jnp.int32)
    distance = jnp.abs(places[:, None] - places[None, :]).astype(jnp.float32)
    raw_scores = raw_scores - slopes[:, None, None] * distance[None]
    key_valid = places < length
    return jnp.where(key_valid[None, None, :], raw_scores, NEGATIVE)


def layer_forward(inputs, length, weights):
    qkv_matrix, out_matrix, gate_matrix, down_matrix, gain_rows, bias_rows = weights
    seq_rows = inputs.shape[0]
    projected = jnp.dot(inputs, qkv_matrix, preferred_element_type=jnp.float32).astype(jnp.bfloat16)
    queries = projected[:, :D]
    key_values = projected[:, D:]
    scores = score_block(
        queries.reshape(seq_rows, HEADS, HEAD),
        key_values[:, :D].reshape(seq_rows, HEADS, HEAD),
        length,
    )
    row_peak = jnp.max(scores, axis=-1, keepdims=True)
    row_exp = jnp.exp(scores - row_peak)
    totals = jnp.sum(row_exp, axis=-1, keepdims=True)
    attn_probs = row_exp / totals
    log_sum = row_peak + jnp.log(totals)
    context = jnp.einsum(
        "hqk,khd->qhd",
        attn_probs.astype(jnp.bfloat16),
        key_values[:, D:].reshape(seq_rows, HEADS, HEAD),
        preferred_element_type=jnp.float32,
    )
    context = context.reshape(seq_rows, D).astype(jnp.bfloat16)
    attended = jnp.dot(context, out_matrix, preferred_element_type=jnp.float32)
    gain_float = gain_rows.astype(jnp.float32)
    bias_float = bias_rows.astype(jnp.float32)
    first_norm, normed_one, inv_one = norm_forward(
        inputs.astype(jnp.float32) + attended, gain_float[0], bias_float[0]
    )
    first_low = first_norm.astype(jnp.bfloat16)
    gate_up = jnp.dot(first_low, gate_matrix, preferred_element_type=jnp.float32)
    gated_rows = (jax.nn.gelu(gate_up[:, :FF], approximate=False) * gate_up[:, FF:]).astype(
        jnp.bfloat16
    )
    down_rows = jnp.dot(gated_rows, down_matrix, preferred_element_type=jnp.float32)
    layer_out, normed_two, inv_two = norm_forward(
        first_norm + down_rows, gain_float[1], bias_float[1]
    )
    stored = (
        inputs,
        queries,
        key_values,
        log_sum,
        context,
        normed_one,
        inv_one,
        first_low,
        gate_up,
        normed_two,
        inv_two,
    )
    return (layer_out, stored)


def layer_backward(upstream, stored, length, weights):
    qkv_matrix, out_matrix, gate_matrix, down_matrix, gain_rows, bias_rows = weights
    (
        inputs,
        queries,
        key_values,
        log_sum,
        context,
        normed_one,
        inv_one,
        first_low,
        gate_up,
        normed_two,
        inv_two,
    ) = stored
    seq_rows = inputs.shape[0]
    gain_float = gain_rows.astype(jnp.float32)
    grad_two, gain_two, bias_two = norm_backward(upstream, normed_two, inv_two, gain_float[1])
    down_grad = grad_two.astype(jnp.bfloat16)
    gate_vals = gate_up[:, :FF]
    up_vals = gate_up[:, FF:]
    gelu_vals = jax.nn.gelu(gate_vals, approximate=False)
    gated_rows = (gelu_vals * up_vals).astype(jnp.bfloat16)
    grad_down_w = jnp.einsum("tf,td->fd", gated_rows, down_grad, preferred_element_type=jnp.float32)
    grad_gated = jnp.einsum("td,fd->tf", down_grad, down_matrix, preferred_element_type=jnp.float32)
    gauss_cdf = 0.5 * (1.0 + lax.erf(gate_vals * 2.0 ** (-0.5)))
    density = jnp.exp(-0.5 * gate_vals * gate_vals) * (2.0 * jnp.pi) ** (-0.5)
    grad_gate = grad_gated * up_vals * (gauss_cdf + gate_vals * density)
    grad_up = grad_gated * gelu_vals
    gate_up_grad = jnp.concatenate([grad_gate, grad_up], axis=1).astype(jnp.bfloat16)
    grad_gu_w = jnp.einsum("td,tf->df", first_low, gate_up_grad, preferred_element_type=jnp.float32)
    grad_first = grad_two + jnp.einsum(
        "tf,df->td", gate_up_grad, gate_matrix, preferred_element_type=jnp.float32
    )
    grad_one, gain_one, bias_one = norm_backward(grad_first, normed_one, inv_one, gain_float[0])
    attn_grad = grad_one.astype(jnp.bfloat16)
    grad_out_w = jnp.einsum("td,te->de", context, attn_grad, preferred_element_type=jnp.float32)
    context_grad = jnp.einsum(
        "te,de->td", attn_grad, out_matrix, preferred_element_type=jnp.float32
    )
    context_grad = context_grad.astype(jnp.bfloat16).reshape(seq_rows, HEADS, HEAD)
    query_heads = queries.reshape(seq_rows, HEADS, HEAD)
    keys_all = key_values[:, :D].reshape(seq_rows, HEADS, HEAD)
    values_all = key_values[:, D:].reshape(seq_rows, HEADS, HEAD)
    scores = score_block(query_heads, keys_all, length)
    attn_probs = jnp.exp(scores - log_sum)
    prob_grad = jnp.einsum(
        "qhd,khd->hqk", context_grad, values_all, preferred_element_type=jnp.float32
    )
    inner_sum = jnp.sum(attn_probs * prob_grad, axis=-1, keepdims=True)
    score_grad = (attn_probs * (prob_grad - inner_sum)).astype(jnp.bfloat16)
    query_grad = jnp.einsum(
        "hqk,khd->qhd", score_grad, keys_all, preferred_element_type=jnp.float32
    ) * HEAD ** (-0.5)
    key_grad = jnp.einsum(
        "hqk,qhd->khd", score_grad, query_heads, preferred_element_type=jnp.float32
    ) * HEAD ** (-0.5)
    value_grad = jnp.einsum(
        "hqk,qhd->khd",
        attn_probs.astype(jnp.bfloat16),
        context_grad,
        preferred_element_type=jnp.float32,
    )
    qkv_grad = jnp.concatenate(
        [
            query_grad.reshape(seq_rows, D),
            key_grad.reshape(seq_rows, D),
            value_grad.reshape(seq_rows, D),
        ],
        axis=1,
    ).astype(jnp.bfloat16)
    grad_qkv_w = jnp.einsum("td,te->de", inputs, qkv_grad, preferred_element_type=jnp.float32)
    input_grad = grad_one + jnp.einsum(
        "te,de->td", qkv_grad, qkv_matrix, preferred_element_type=jnp.float32
    )
    grad_terms = (
        grad_qkv_w,
        grad_out_w,
        grad_gu_w,
        grad_down_w,
        jnp.stack([gain_one, gain_two]),
        jnp.stack([bias_one, bias_two]),
    )
    return (input_grad, grad_terms)


def store_slot(slot_index, active, buffer, new_value):
    previous = lax.dynamic_index_in_dim(buffer, slot_index, 0, keepdims=False)
    return lax.dynamic_update_index_in_dim(
        buffer, jnp.where(active, new_value, previous), slot_index, 0
    )


def shards(tokens, lengths, w_qkv, w_out, w_gate_up, w_down, norm_gain, norm_bias, cotangent):
    section_index = lax.axis_index("section")
    window = lax.axis_index("dp")
    micro_count = tokens.shape[0]
    seq_rows = tokens.shape[1]
    forward_weights = (
        lax.all_gather(w_qkv[0].astype(jnp.bfloat16), "dp", axis=0, tiled=True),
        lax.all_gather(w_out[0].astype(jnp.bfloat16), "dp", axis=0, tiled=True),
        lax.all_gather(w_gate_up[0].astype(jnp.bfloat16), "dp", axis=0, tiled=True),
        lax.all_gather(w_down[0].astype(jnp.bfloat16), "dp", axis=0, tiled=True),
        lax.all_gather(norm_gain[0].astype(jnp.bfloat16), "dp", axis=1, tiled=True),
        lax.all_gather(norm_bias[0].astype(jnp.bfloat16), "dp", axis=1, tiled=True),
    )

    def length_of(slot_index):
        length_row = lax.dynamic_index_in_dim(lengths, slot_index, 0, keepdims=False)
        return lax.dynamic_index_in_dim(length_row, window, 0, keepdims=False)

    def slot_zeros(shape, dtype):
        return jnp.zeros((micro_count,) + shape, dtype)

    stash_init = (
        slot_zeros((seq_rows, D), jnp.bfloat16),
        slot_zeros((seq_rows, D), jnp.bfloat16),
        slot_zeros((seq_rows, 2 * D), jnp.bfloat16),
        slot_zeros((HEADS, seq_rows, 1), jnp.float32),
        slot_zeros((seq_rows, D), jnp.bfloat16),
        slot_zeros((seq_rows, D), jnp.float32),
        slot_zeros((seq_rows, 1), jnp.float32),
        slot_zeros((seq_rows, D), jnp.bfloat16),
        slot_zeros((seq_rows, 2 * FF), jnp.float32),
        slot_zeros((seq_rows, D), jnp.float32),
        slot_zeros((seq_rows, 1), jnp.float32),
        slot_zeros((seq_rows, D), jnp.bfloat16),
    )

    def forward_tick(carry, tick_now):
        arrived, stash = carry
        offset = tick_now - section_index
        slot_index = jnp.clip(offset, 0, micro_count - 1)
        active = (offset >= 0) & (offset < micro_count)
        own_input = lax.dynamic_index_in_dim(tokens, slot_index, 0, keepdims=False)
        layer_input = jnp.where(section_index == 0, own_input, arrived)
        layer_out, stored = layer_forward(layer_input, length_of(slot_index), forward_weights)
        sent_rows = layer_out.astype(jnp.bfloat16)
        passed = shifted(sent_rows, "section", 1)
        stash = tuple(
            (
                store_slot(slot_index, active, buffer, new_value)
                for buffer, new_value in zip(stash, stored + (sent_rows,))
            )
        )
        return ((passed, stash), None)

    tick_list = jnp.arange(micro_count + 1, dtype=jnp.int32)
    start_rows = jnp.zeros((seq_rows, D), jnp.bfloat16)
    (unused, stash), unused_out = lax.scan(forward_tick, (start_rows, stash_init), tick_list)
    backward_weights = (
        lax.all_gather(w_qkv[0].astype(jnp.bfloat16), "dp", axis=0, tiled=True),
        lax.all_gather(w_out[0].astype(jnp.bfloat16), "dp", axis=0, tiled=True),
        lax.all_gather(w_gate_up[0].astype(jnp.bfloat16), "dp", axis=0, tiled=True),
        lax.all_gather(w_down[0].astype(jnp.bfloat16), "dp", axis=0, tiled=True),
        lax.all_gather(norm_gain[0].astype(jnp.bfloat16), "dp", axis=1, tiled=True),
        lax.all_gather(norm_bias[0].astype(jnp.bfloat16), "dp", axis=1, tiled=True),
    )

    def backward_tick(carry, tick_now):
        arrived, summed, grads_in = carry
        offset = tick_now - 1 + section_index
        slot_index = jnp.clip(offset, 0, micro_count - 1)
        active = (offset >= 0) & (offset < micro_count)
        cot_rows = lax.dynamic_index_in_dim(cotangent, slot_index, 0, keepdims=False).astype(
            jnp.float32
        )
        upstream = jnp.where(section_index == 1, cot_rows, arrived.astype(jnp.float32))
        stored = tuple(
            (
                lax.dynamic_index_in_dim(buffer, slot_index, 0, keepdims=False)
                for buffer in stash[:-1]
            )
        )
        input_grad, grad_terms = layer_backward(
            upstream, stored, length_of(slot_index), backward_weights
        )
        weight_flag = active.astype(jnp.float32)
        masked = tuple((term * weight_flag for term in grad_terms))
        summed = tuple((left + right for left, right in zip(summed, masked)))
        passed = shifted(input_grad.astype(jnp.bfloat16), "section", -1)
        grads_in = store_slot(slot_index, active, grads_in, input_grad)
        return ((passed, summed, grads_in), None)

    summed_init = (
        jnp.zeros((D, 3 * D), jnp.float32),
        jnp.zeros((D, D), jnp.float32),
        jnp.zeros((D, 2 * FF), jnp.float32),
        jnp.zeros((FF, D), jnp.float32),
        jnp.zeros((2, D), jnp.float32),
        jnp.zeros((2, D), jnp.float32),
    )
    grads_init = jnp.zeros((micro_count, seq_rows, D), jnp.float32)
    (unused_back, summed, grads_in), unused_list = lax.scan(
        backward_tick, (start_rows, summed_init, grads_init), tick_list
    )
    attn_share = (
        lax.psum_scatter(summed[0], "dp", scatter_dimension=0, tiled=True),
        lax.psum_scatter(summed[1], "dp", scatter_dimension=0, tiled=True),
        lax.psum_scatter(summed[4], "dp", scatter_dimension=1, tiled=True),
        lax.psum_scatter(summed[5], "dp", scatter_dimension=1, tiled=True),
    )
    gate_share = lax.psum_scatter(summed[2], "dp", scatter_dimension=0, tiled=True)
    down_share = lax.psum_scatter(summed[3], "dp", scatter_dimension=0, tiled=True)
    shares = (attn_share[0], attn_share[1], gate_share, down_share, attn_share[2], attn_share[3])
    return (
        stash[-1][None],
        grads_in[None],
        shares[0][None],
        shares[1][None],
        shares[2][None],
        shares[3][None],
        shares[4][None],
        shares[5][None],
    )


def solution(mesh):
    return jax.shard_map(
        shards,
        mesh=mesh,
        in_specs=(
            P(None, "dp", None),
            P(),
            P("section", "dp", None),
            P("section", "dp", None),
            P("section", "dp", None),
            P("section", "dp", None),
            P("section", None, "dp"),
            P("section", None, "dp"),
            P(None, "dp", None),
        ),
        out_specs=(
            P("section", None, "dp", None),
            P("section", None, "dp", None),
            P("section", "dp", None),
            P("section", "dp", None),
            P("section", "dp", None),
            P("section", "dp", None),
            P("section", None, "dp"),
            P("section", None, "dp"),
        ),
        check_vma=False,
    )
```

profile of v0, /device:TPU:0, one launch (start us, length us, event | category | flops | bytes accessed | tf_op | source)
XLA Modules:
  0.0 1286.7 jit_solution(15711562108209963430)
XLA Ops:
  13.9 24.4 %all-gather.2 = bf16[1,2,768]{1,0,2:T(2,128)(2,1)S(1)} all-gather(bf16[1,2,48]{1,0,2:T(2,128)(2,1)S(1)} %copy.83), channel_id=4, replica_groups=mesh['section'=2,'dp'=16] {'dp'}, dimensions={2}, use_global_device_ids=true | all-gather | bytes 3264 | tf_op jit(solution)/shard_map/all_gather | solution.py:207
  39.1 18.7 %all-gather.3 = bf16[1,2,768]{1,0,2:T(2,128)(2,1)S(1)} all-gather(bf16[1,2,48]{1,0,2:T(2,128)(2,1)S(1)} %copy.85), channel_id=5, replica_groups=mesh['section'=2,'dp'=16] {'dp'}, dimensions={2}, use_global_device_ids=true | all-gather | bytes 3264 | tf_op jit(solution)/shard_map/all_gather | solution.py:208
  58.7 42.9 %all-gather.11.cloned.1.call-done = bf16[1,768,2304]{2,1,0:T(8,128)(2,1)} async-done(((bf16[1,48,2304]{2,1,0:T(8,128)(2,1)}), bf16[1,768,2304]{2,1,0:T(8,128)(2,1)}) %all-gather.11.cloned.1.call-update) | async-done | bytes 3538960 | tf_op jit(solution)/shard_map/all_gather | solution.py:203
  101.6 55.1 %all-gather.17.cloned.1.call-done = bf16[1,3072,768]{2,1,0:T(8,128)(2,1)} async-done(((bf16[1,192,768]{2,1,0:T(8,128)(2,1)}), bf16[1,3072,768]{2,1,0:T(8,128)(2,1)}) %all-gather.17.cloned.1.call-update) | async-done | bytes 4718608 | tf_op jit(solution)/shard_map/all_gather | solution.py:206
  156.7 82.7 %all-gather.15.cloned.1.call-done = bf16[1,768,6144]{2,1,0:T(8,128)(2,1)} async-done(((bf16[1,48,6144]{2,1,0:T(8,128)(2,1)}), bf16[1,768,6144]{2,1,0:T(8,128)(2,1)}) %all-gather.15.cloned.1.call-update) | async-done | bytes 9437200 | tf_op jit(solution)/shard_map/all_gather | solution.py:205
  251.1 6.1 broadcast_in_dim.183
  257.3 182.2 %while.65 = (s32[]{:T(128)}, bf16[256,768]{1,0:T(8,128)(2,1)}, bf16[2,256,768]{2,1,0:T(8,128)(2,1)}, bf16[2,256,768]{2,1,0:T(8,128)(2,1)}, bf16[2,256,1536]{2,1,...) while((s32[]{:T(128)}, bf16[256,768]{1,0:T(8,128)(2,1)}, ...), condition=%wide.region_7.8_spmd, body=%wide.region_0.7_spmd.sunk | while | flops 5104144384 | bytes 246386960 | solution.py:253
  266.4 1.9 bitcast_dynamic-update-slice_fusion.14
  268.4 3.1 convolution_convert_fusion.4
  273.1 2.0 fusion.198
  279.3 9.0 bitcast_dynamic-update-slice_fusion.15
  288.3 15.4 %fusion.202 = (f32[256]{0:T(256)S(1)}, f32[256,768]{1,0:T(8,128)S(1)}) fusion(bf16[3072,768]{1,0:T(8,128)(2,1)} %get-tuple-element.1968, f32[256,6144]{1,0:T(8,128)} %get-tuple-element.1817, f32[768]{0:T(1024)S(1)} %get-tuple-element.1814, f32[768]{0:T(1024)S(1)} %get-tuple-element.1815, f32[256]{0:T(256)S(1)} %add_rsqrt_fusion.4, ...), kind=kOutput, calls=%fused_computation.222.clone.1 | convolution fusion | flops 1261043456 | bytes 12592128 | tf_op jit(solution)/shard_map/while/body/eval_jaxpr/dot_general | solution.py:84
  305.1 4.4 collective-permute-start
  314.6 2.6 bitcast_dynamic-update-slice_fusion.18
  327.0 1.9 bitcast_dynamic-update-slice_fusion.14
  328.9 3.1 convolution_convert_fusion.4
  333.6 2.0 fusion.198
  339.9 9.0 bitcast_dynamic-update-slice_fusion.15
  348.9 15.3 %fusion.202 = (f32[256]{0:T(256)S(1)}, f32[256,768]{1,0:T(8,128)S(1)}) fusion(bf16[3072,768]{1,0:T(8,128)(2,1)} %get-tuple-element.1968, f32[256,6144]{1,0:T(8,128)} %get-tuple-element.1817, f32[768]{0:T(1024)S(1)} %get-tuple-element.1814, f32[768]{0:T(1024)S(1)} %get-tuple-element.1815, f32[256]{0:T(256)S(1)} %add_rsqrt_fusion.4, ...), kind=kOutput, calls=%fused_computation.222.clone.1 | convolution fusion | flops 1261043456 | bytes 12592128 | tf_op jit(solution)/shard_map/while/body/eval_jaxpr/dot_general | solution.py:84
  365.7 5.4 collective-permute-start
  376.2 2.6 bitcast_dynamic-update-slice_fusion.18
  387.9 1.9 bitcast_dynamic-update-slice_fusion.14
  389.8 3.1 convolution_convert_fusion.4
  394.5 2.0 fusion.198
  400.7 9.0 bitcast_dynamic-update-slice_fusion.15
  409.8 15.4 %fusion.202 = (f32[256]{0:T(256)S(1)}, f32[256,768]{1,0:T(8,128)S(1)}) fusion(bf16[3072,768]{1,0:T(8,128)(2,1)} %get-tuple-element.1968, f32[256,6144]{1,0:T(8,128)} %get-tuple-element.1817, f32[768]{0:T(1024)S(1)} %get-tuple-element.1814, f32[768]{0:T(1024)S(1)} %get-tuple-element.1815, f32[256]{0:T(256)S(1)} %add_rsqrt_fusion.4, ...), kind=kOutput, calls=%fused_computation.222.clone.1 | convolution fusion | flops 1261043456 | bytes 12592128 | tf_op jit(solution)/shard_map/while/body/eval_jaxpr/dot_general | solution.py:84
  426.6 5.2 collective-permute-start
  436.9 2.6 bitcast_dynamic-update-slice_fusion.18
  442.0 244.6 %while.66 = (s32[]{:T(128)}, bf16[256,768]{1,0:T(8,128)(2,1)}, f32[768,2304]{1,0:T(8,128)}, f32[768,768]{1,0:T(8,128)}, f32[768,6144]{1,0:T(8,128)}, /*index=5*/...) while((s32[]{:T(128)}, bf16[256,768]{1,0:T(8,128)(2,1)}, ...), condition=%wide.region_18.19_spmd.clone, body=%wide.region_8.18_spmd.clone.sunk | while | flops 10294599680 | bytes 342882656 | solution.py:297
  451.5 2.3 fusion.225
  459.2 4.1 dynamic-slice_bitcast_fusion.4
  465.1 10.6 multiply_convert_fusion.8
  475.8 3.4 fusion.227
  487.2 2.1 fusion.234
  493.2 7.3 select_add_fusion.11
  500.4 5.1 select_add_fusion.8
  505.6 8.4 select_add_fusion.10
  514.1 1.9 select_add_fusion.9
  525.4 2.3 fusion.225
  533.1 4.1 dynamic-slice_bitcast_fusion.4
  539.1 10.6 multiply_convert_fusion.8
  549.8 3.4 fusion.227
  561.1 2.1 fusion.234
  566.1 2.1 bitcast_dynamic-update-slice_fusion.19
  568.3 10.0 select_add_fusion.11
  578.3 7.2 select_add_fusion.8
  585.6 12.1 select_add_fusion.10
  597.7 3.5 select_add_fusion.9
  610.8 2.3 fusion.225
  618.5 4.1 dynamic-slice_bitcast_fusion.4
  624.4 10.6 multiply_convert_fusion.8
  635.1 3.4 fusion.227
  646.4 2.1 fusion.234
  651.5 2.1 bitcast_dynamic-update-slice_fusion.19
  653.6 10.0 select_add_fusion.11
  663.6 7.2 select_add_fusion.8
  670.9 12.1 select_add_fusion.10
  683.1 3.5 select_add_fusion.9
  692.8 52.8 %reduce-scatter.21.cloned.1.call-done = f32[48,2]{1,0:T(8,128)} async-done(((f32[768,2]{1,0:T(8,128)}), f32[48,2]{1,0:T(8,128)}) %reduce-scatter.21.cloned.1.call-update) | async-done | bytes 400
  747.0 57.0 %reduce-scatter.19.cloned.1.call-done = f32[48,2]{1,0:T(8,128)} async-done(((f32[768,2]{1,0:T(8,128)}), f32[48,2]{1,0:T(8,128)}) %reduce-scatter.19.cloned.1.call-update) | async-done | bytes 400
  805.4 65.0 %reduce-scatter.13.cloned.1.call-done = f32[48,768]{1,0:T(8,128)} async-done(((f32[768,768]{1,0:T(8,128)}), f32[48,768]{1,0:T(8,128)}) %reduce-scatter.13.cloned.1.call-update) | async-done | bytes 147472 | tf_op jit(solution)/shard_map/reduce_scatter | solution.py:302
  870.4 94.1 %reduce-scatter.11.cloned.1.call-done = f32[48,2304]{1,0:T(8,128)} async-done(((f32[768,2304]{1,0:T(8,128)}), f32[48,2304]{1,0:T(8,128)}) %reduce-scatter.11.cloned.1.call-update) | async-done | bytes 442384 | tf_op jit(solution)/shard_map/reduce_scatter | solution.py:301
  964.5 115.6 %reduce-scatter.17.cloned.1.call-done = f32[192,768]{1,0:T(8,128)} async-done(((f32[3072,768]{1,0:T(8,128)}), f32[192,768]{1,0:T(8,128)}) %reduce-scatter.17.cloned.1.call-update) | async-done | bytes 589840 | tf_op jit(solution)/shard_map/reduce_scatter | solution.py:307
  1080.2 199.7 %reduce-scatter.15.cloned.1.call-done = f32[48,6144]{1,0:T(8,128)} async-done(((f32[768,6144]{1,0:T(8,128)}), f32[48,6144]{1,0:T(8,128)}) %reduce-scatter.15.cloned.1.call-update) | async-done | bytes 1179664 | tf_op jit(solution)/shard_map/reduce_scatter | solution.py:306
  (678 shorter events, 174.1 us)
Async XLA Ops:
  7.2 51.5 %all-gather.13.cloned.1.call-start = ((), (), s32[]{:S(2)}) async-start(), calls=%async_computation.11 | async-start | bytes 1253376 | tf_op jit(solution)/shard_map/all_gather | solution.py:204
  8.9 92.7 %all-gather.11.cloned.1.call-start = ((), (), s32[]{:S(2)}) async-start(), calls=%async_computation.10 | async-start | bytes 3760128 | tf_op jit(solution)/shard_map/all_gather | solution.py:203
  10.7 146.0 %all-gather.17.cloned.1.call-start = ((), (), s32[]{:S(2)}) async-start(), calls=%async_computation.13 | async-start | bytes 5013504 | tf_op jit(solution)/shard_map/all_gather | solution.py:206
  12.6 226.8 %all-gather.15.cloned.1.call-start = ((), (), s32[]{:S(2)}) async-start(), calls=%async_computation.12 | async-start | bytes 10027008 | tf_op jit(solution)/shard_map/all_gather | solution.py:205
  13.5 732.1 %reduce-scatter.21.cloned.1.call-start = ((), (), s32[]{:S(2)}) async-start(), calls=%async_computation.15 | async-start | bytes 417792
  288.3 15.4 %copy-start = (f32[2,256,6144]{2,1,0:T(8,128)}, f32[2,256,6144]{2,1,0:T(8,128)S(1)}, u32[]{:S(2)}) copy-start(f32[2,256,6144]{2,1,0:T(8,128)S(1)} %get-tuple-element.1953) | copy-start | bytes 37748740 | tf_op jit(solution)/shard_map/while
  288.3 15.7 %copy-start.38 = (f32[768]{0:T(1024)S(1)}, f32[768]{0:T(1024)}, u32[]{:S(2)}) copy-start(f32[768]{0:T(1024)} %get-tuple-element.1805) | copy-start | bytes 9220 | tf_op jit(solution)/shard_map/while
  288.3 15.7 %copy-start.39 = (f32[768]{0:T(1024)S(1)}, f32[768]{0:T(1024)}, u32[]{:S(2)}) copy-start(f32[768]{0:T(1024)} %get-tuple-element.1806) | copy-start | bytes 9220 | tf_op jit(solution)/shard_map/while
  288.3 21.2 %copy-start.26 = (bf16[2,256,768]{2,1,0:T(8,128)(2,1)S(1)}, bf16[2,256,768]{2,1,0:T(8,128)(2,1)}, u32[]{:S(2)}) copy-start(bf16[2,256,768]{2,1,0:T(8,128)(2,1)} %get-tuple-element.1917) | copy-start | bytes 2359300 | tf_op jit(solution)/shard_map/while
  288.3 21.3 %copy-start.20 = (bf16[2,256,768]{2,1,0:T(8,128)(2,1)S(1)}, bf16[2,256,768]{2,1,0:T(8,128)(2,1)}, u32[]{:S(2)}) copy-start(bf16[2,256,768]{2,1,0:T(8,128)(2,1)} %get-tuple-element.1923) | copy-start | bytes 2359300 | tf_op jit(solution)/shard_map/while
  304.0 8.5 copy-start.41
  305.1 12.7 collective-permute-start
  348.9 15.4 %copy-start = (f32[2,256,6144]{2,1,0:T(8,128)}, f32[2,256,6144]{2,1,0:T(8,128)S(1)}, u32[]{:S(2)}) copy-start(f32[2,256,6144]{2,1,0:T(8,128)S(1)} %get-tuple-element.1953) | copy-start | bytes 37748740 | tf_op jit(solution)/shard_map/while
  348.9 15.7 %copy-start.38 = (f32[768]{0:T(1024)S(1)}, f32[768]{0:T(1024)}, u32[]{:S(2)}) copy-start(f32[768]{0:T(1024)} %get-tuple-element.1805) | copy-start | bytes 9220 | tf_op jit(solution)/shard_map/while
  348.9 15.7 %copy-start.39 = (f32[768]{0:T(1024)S(1)}, f32[768]{0:T(1024)}, u32[]{:S(2)}) copy-start(f32[768]{0:T(1024)} %get-tuple-element.1806) | copy-start | bytes 9220 | tf_op jit(solution)/shard_map/while
  348.9 22.2 %copy-start.26 = (bf16[2,256,768]{2,1,0:T(8,128)(2,1)S(1)}, bf16[2,256,768]{2,1,0:T(8,128)(2,1)}, u32[]{:S(2)}) copy-start(bf16[2,256,768]{2,1,0:T(8,128)(2,1)} %get-tuple-element.1917) | copy-start | bytes 2359300 | tf_op jit(solution)/shard_map/while
  348.9 22.2 %copy-start.20 = (bf16[2,256,768]{2,1,0:T(8,128)(2,1)S(1)}, bf16[2,256,768]{2,1,0:T(8,128)(2,1)}, u32[]{:S(2)}) copy-start(bf16[2,256,768]{2,1,0:T(8,128)(2,1)} %get-tuple-element.1923) | copy-start | bytes 2359300 | tf_op jit(solution)/shard_map/while
  364.5 9.5 copy-start.41
  365.7 13.0 %collective-permute-start = (bf16[256,768]{1,0:T(8,128)(2,1)}, bf16[256,768]{1,0:T(8,128)(2,1)}, u32[]{:S(2)}, u32[]{:S(2)}) collective-permute-start(bf16[256,768]{1,0:T(8,128)(2,1)} %get-tuple-element.1820), channel_id=1, source_target_pairs={{0,16},{1,17},{2,18},{3,19},{4,20},{5,21},{6,22},{7,23},{8,24},{9,... | collective-permute-start | bytes 1179656 | tf_op jit(solution)/shard_map/while/body/eval_jaxpr/ppermute | solution.py:17
  409.7 15.4 %copy-start = (f32[2,256,6144]{2,1,0:T(8,128)}, f32[2,256,6144]{2,1,0:T(8,128)S(1)}, u32[]{:S(2)}) copy-start(f32[2,256,6144]{2,1,0:T(8,128)S(1)} %get-tuple-element.1953) | copy-start | bytes 37748740 | tf_op jit(solution)/shard_map/while
  409.7 15.7 %copy-start.38 = (f32[768]{0:T(1024)S(1)}, f32[768]{0:T(1024)}, u32[]{:S(2)}) copy-start(f32[768]{0:T(1024)} %get-tuple-element.1805) | copy-start | bytes 9220 | tf_op jit(solution)/shard_map/while
  409.7 15.7 %copy-start.39 = (f32[768]{0:T(1024)S(1)}, f32[768]{0:T(1024)}, u32[]{:S(2)}) copy-start(f32[768]{0:T(1024)} %get-tuple-element.1806) | copy-start | bytes 9220 | tf_op jit(solution)/shard_map/while
  409.8 22.1 %copy-start.26 = (bf16[2,256,768]{2,1,0:T(8,128)(2,1)S(1)}, bf16[2,256,768]{2,1,0:T(8,128)(2,1)}, u32[]{:S(2)}) copy-start(bf16[2,256,768]{2,1,0:T(8,128)(2,1)} %get-tuple-element.1917) | copy-start | bytes 2359300 | tf_op jit(solution)/shard_map/while
  409.8 22.1 %copy-start.20 = (bf16[2,256,768]{2,1,0:T(8,128)(2,1)S(1)}, bf16[2,256,768]{2,1,0:T(8,128)(2,1)}, u32[]{:S(2)}) copy-start(bf16[2,256,768]{2,1,0:T(8,128)(2,1)} %get-tuple-element.1923) | copy-start | bytes 2359300 | tf_op jit(solution)/shard_map/while
  425.4 9.4 copy-start.41
  426.6 12.9 %collective-permute-start = (bf16[256,768]{1,0:T(8,128)(2,1)}, bf16[256,768]{1,0:T(8,128)(2,1)}, u32[]{:S(2)}, u32[]{:S(2)}) collective-permute-start(bf16[256,768]{1,0:T(8,128)(2,1)} %get-tuple-element.1820), channel_id=1, source_target_pairs={{0,16},{1,17},{2,18},{3,19},{4,20},{5,21},{6,22},{7,23},{8,24},{9,... | collective-permute-start | bytes 1179656 | tf_op jit(solution)/shard_map/while/body/eval_jaxpr/ppermute | solution.py:17
  463.3 12.5 copy-start.1
  463.4 12.4 slice-start.3
  465.1 10.7 copy-start.7
  465.1 10.7 slice-start.4
  465.1 10.7 slice-start.5
  465.1 10.7 copy-start.13
  465.1 10.7 copy-start.40
  489.3 26.7 %collective-permute-start.1 = (bf16[256,768]{1,0:T(8,128)(2,1)}, bf16[256,768]{1,0:T(8,128)(2,1)}, u32[]{:S(2)}, u32[]{:S(2)}) collective-permute-start(bf16[256,768]{1,0:T(8,128)(2,1)} %get-tuple-element.1876), channel_id=1, source_target_pairs={{16,0},{17,1},{18,2},{19,3},{20,4},{21,5},{22,6},{23,7},{24,8},{25... | collective-permute-start | bytes 1179656 | tf_op jit(solution)/shard_map/while/body/eval_jaxpr/ppermute | solution.py:17
  505.6 8.5 copy-start.25
  537.3 12.5 copy-start.1
  537.3 12.4 slice-start.3
  539.0 10.7 copy-start.7
  539.1 10.7 slice-start.4
  539.1 10.7 slice-start.5
  539.1 10.7 copy-start.13
  539.1 10.7 copy-start.40
  563.3 38.0 %collective-permute-start.1 = (bf16[256,768]{1,0:T(8,128)(2,1)}, bf16[256,768]{1,0:T(8,128)(2,1)}, u32[]{:S(2)}, u32[]{:S(2)}) collective-permute-start(bf16[256,768]{1,0:T(8,128)(2,1)} %get-tuple-element.1876), channel_id=1, source_target_pairs={{16,0},{17,1},{18,2},{19,3},{20,4},{21,5},{22,6},{23,7},{24,8},{25... | collective-permute-start | bytes 1179656 | tf_op jit(solution)/shard_map/while/body/eval_jaxpr/ppermute | solution.py:17
  568.3 10.0 copy-start.19
  585.5 12.2 copy-start.42
  585.5 12.1 copy-start.44
  585.5 12.2 copy-start.25
  622.6 12.5 copy-start.1
  622.7 12.4 slice-start.3
  624.4 10.7 copy-start.7
  624.4 10.7 slice-start.4
  624.4 10.7 slice-start.5
  624.4 10.7 copy-start.13
  624.4 10.7 copy-start.40
  648.6 38.0 %collective-permute-start.1 = (bf16[256,768]{1,0:T(8,128)(2,1)}, bf16[256,768]{1,0:T(8,128)(2,1)}, u32[]{:S(2)}, u32[]{:S(2)}) collective-permute-start(bf16[256,768]{1,0:T(8,128)(2,1)} %get-tuple-element.1876), channel_id=1, source_target_pairs={{16,0},{17,1},{18,2},{19,3},{20,4},{21,5},{22,6},{23,7},{24,8},{25... | collective-permute-start | bytes 1179656 | tf_op jit(solution)/shard_map/while/body/eval_jaxpr/ppermute | solution.py:17
  653.6 10.0 copy-start.19
  670.8 12.2 copy-start.42
  670.9 12.1 copy-start.44
  670.9 12.2 copy-start.25
  688.3 115.7 %reduce-scatter.19.cloned.1.call-start = ((), (), s32[]{:S(2)}) async-start(), calls=%async_computation.14 | async-start | bytes 417792
  690.0 180.4 %reduce-scatter.13.cloned.1.call-start = ((), (), s32[]{:S(2)}) async-start(), calls=%async_computation.7 | async-start | bytes 2506752 | tf_op jit(solution)/shard_map/reduce_scatter | solution.py:302
  690.8 273.8 %reduce-scatter.11.cloned.1.call-start = ((), (), s32[]{:S(2)}) async-start(), calls=%async_computation.6 | async-start | bytes 7520256 | tf_op jit(solution)/shard_map/reduce_scatter | solution.py:301
  691.5 388.6 %reduce-scatter.17.cloned.1.call-start = ((), (), s32[]{:S(2)}) async-start(), calls=%async_computation.9 | async-start | bytes 10027008 | tf_op jit(solution)/shard_map/reduce_scatter | solution.py:307
  692.3 587.6 %reduce-scatter.15.cloned.1.call-start = ((), (), s32[]{:S(2)}) async-start(), calls=%async_computation.8 | async-start | bytes 20054016 | tf_op jit(solution)/shard_map/reduce_scatter | solution.py:306
  (148 other events, 540.7 us)
Sparse Core Ops, SparseCore 0:
  10.9 42.0 all-gather.12
  55.9 45.6 all-gather.10
  104.4 52.2 all-gather.16
  159.4 79.9 all-gather.14
  688.4 57.1 reduce-scatter.20
  749.4 54.5 reduce-scatter.18
  808.4 62.0 reduce-scatter.12
  875.5 88.9 reduce-scatter.10
  969.2 110.8 reduce-scatter.16
  1085.2 194.5 reduce-scatter.14
where the time goes:
time: 1290 us
  waiting for transfers between devices  768 us (60%)
  matrix products  244 us (19%)
  local copies, waits for them, and re-layouts  119 us (9%)
  other arithmetic  71.3 us (6%)
  blocking collectives  43 us (3%)
  starting transfers between devices  19.6 us (2%)
  between operations  14.3 us (1%)
    reduce_scatter x1, waiting for transfers between devices, shards(): lax.psum_scatter(summed[2], 'dp', scatter_dimension=0, tiled=True)  200 us
    reduce_scatter x1, waiting for transfers between devices, shards(): lax.psum_scatter(summed[3], 'dp', scatter_dimension=0, tiled=True)  116 us
    unnamed x12, waiting for transfers between devices  112 us
    reduce_scatter x1, waiting for transfers between devices, shards(): lax.psum_scatter(summed[0], 'dp', scatter_dimension=0, tiled=True)  94.1 us
    all_gather x1, waiting for transfers between devices, shards(): lax.all_gather(w_gate_up[0].astype(jnp.bfloat16), 'dp', axis=0, tiled=True)  82.7 us
    reduce_scatter x1, waiting for transfers between devices, shards(): lax.psum_scatter(summed[1], 'dp', scatter_dimension=0, tiled=True)  65 us
    all_gather x1, waiting for transfers between devices, shards(): lax.all_gather(w_down[0].astype(jnp.bfloat16), 'dp', axis=0, tiled=True)  55.1 us
    dot_general x3, matrix products, layer_forward(): jnp.dot(gated_rows, down_matrix, preferred_element_type=jnp.float32)  46.1 us
  transfers between devices with their start and end apart: 16, of which 10 were waited for; matrix products, arithmetic and copies ran while one was open for 9% of the time, Pallas kernels for 0%

commit v1 on v0

--- a/solution.py
+++ b/solution.py
@@ -1,3 +1,4 @@
+import functools
 import jax
 import jax.numpy as jnp
 from jax import lax
@@ -9,6 +10,26 @@
 FF = 3072
 EPSILON = 1e-05
 NEGATIVE = -1e30
+
+
+def _serve_views(z, axis_key, array_axis):
+    view_out = jax.lax.axis_size(axis_key)
+    m_next = jax.lax.axis_index(axis_key)
+    later, all_rows = (view_out, m_next)
+    arr_out, aux = (z, 1)
+    while aux < later:
+        made = []
+        for num in [*range(later)]:
+            made.append((num, num ^ aux))
+        res = jax.lax.ppermute(arr_out, axis_key, perm=made)
+        placed = jnp.concatenate([arr_out, res], axis=array_axis)
+        earlier = jnp.concatenate([res, arr_out], axis=array_axis)
+        arr_out = jnp.where(all_rows & aux == 0, placed, earlier)
+        aux = 2 * aux
+    return arr_out
+
+
+return_all_islands = functools.partial(_serve_views, axis_key="dp", array_axis=0)
 
 
 def shifted(shard, axis, by):
@@ -202,7 +223,7 @@
     forward_weights = (
         lax.all_gather(w_qkv[0].astype(jnp.bfloat16), "dp", axis=0, tiled=True),
         lax.all_gather(w_out[0].astype(jnp.bfloat16), "dp", axis=0, tiled=True),
-        lax.all_gather(w_gate_up[0].astype(jnp.bfloat16), "dp", axis=0, tiled=True),
+        return_all_islands(w_gate_up[0].astype(jnp.bfloat16)),
         lax.all_gather(w_down[0].astype(jnp.bfloat16), "dp", axis=0, tiled=True),
         lax.all_gather(norm_gain[0].astype(jnp.bfloat16), "dp", axis=1, tiled=True),
         lax.all_gather(norm_bias[0].astype(jnp.bfloat16), "dp", axis=1, tiled=True),

time: 1290 us -> 1460 us (1.13)
  blocking collectives: 43 us -> 264 us
  waiting for transfers between devices: 768 us -> 690 us
  other arithmetic: 71.3 us -> 94.7 us
    all_gather x1, blocking collectives: 18.7 us -> 143 us  [shards(): lax.all_gather(norm_bias[0].astype(jnp.bfloat16), 'dp', axis=1, tiled=True)]
    ppermute x0 -> x4, waiting for transfers between devices: none -> 104 us  [_serve_views(): res = jax.lax.ppermute(arr_out, axis_key, perm=made)]
    all_gather x1, blocking collectives: 24.4 us -> 121 us  [shards(): lax.all_gather(norm_gain[0].astype(jnp.bfloat16), 'dp', axis=1, tiled=True)]
    all_gather x1, waiting for transfers between devices: 82.7 us -> 0.01 us  [shards(): lax.all_gather(w_gate_up[0].astype(jnp.bfloat16), 'dp', axis=0, tiled=True)]
    all_gather x1, waiting for transfers between devices: 55.1 us -> 0.01 us  [shards(): lax.all_gather(w_down[0].astype(jnp.bfloat16), 'dp', axis=0, tiled=True)]
    all_gather x1, waiting for transfers between devices: 42.9 us -> 0.01 us  [shards(): lax.all_gather(w_qkv[0].astype(jnp.bfloat16), 'dp', axis=0, tiled=True)]
    select_n x0 -> x4, other arithmetic: none -> 20.8 us  [_serve_views(): arr_out = jnp.where(all_rows & aux == 0, placed, earlier)]
    dot_general x3, matrix products: 10.2 us -> 26 us  [layer_backward(): jnp.einsum('tf,df->td', gate_up_grad, gate_matrix, preferred_element_type...]
  transfers between devices with their start and end apart: 16 -> 20, of which waited for: 10 -> 9; matrix products, arithmetic and copies ran while one was open for 9% -> 20% of each run, Pallas kernels for 0% -> 0%
where the time goes in v1:
time: 1460 us
  waiting for transfers between devices  690 us (47%)
  blocking collectives  264 us (18%)
  matrix products  240 us (16%)
  local copies, waits for them, and re-layouts  126 us (9%)
  other arithmetic  94.7 us (6%)
  starting transfers between devices  23.8 us (2%)
    reduce_scatter x1, waiting for transfers between devices, shards(): lax.psum_scatter(summed[2], 'dp', scatter_dimension=0, tiled=True)  200 us
    all_gather x1, blocking collectives, shards(): lax.all_gather(norm_bias[0].astype(jnp.bfloat16), 'dp', axis=1, tiled=True)  143 us
    all_gather x1, blocking collectives, shards(): lax.all_gather(norm_gain[0].astype(jnp.bfloat16), 'dp', axis=1, tiled=True)  121 us
    reduce_scatter x1, waiting for transfers between devices, shards(): lax.psum_scatter(summed[3], 'dp', scatter_dimension=0, tiled=True)  116 us
    unnamed x12, waiting for transfers between devices  112 us
    ppermute x4, waiting for transfers between devices, _serve_views(): res = jax.lax.ppermute(arr_out, axis_key, perm=made)  104 us
    reduce_scatter x1, waiting for transfers between devices, shards(): lax.psum_scatter(summed[0], 'dp', scatter_dimension=0, tiled=True)  94.2 us
    reduce_scatter x1, waiting for transfers between devices, shards(): lax.psum_scatter(summed[1], 'dp', scatter_dimension=0, tiled=True)  65 us
  transfers between devices with their start and end apart: 20, of which 9 were waited for; matrix products, arithmetic and copies ran while one was open for 20% of the time, Pallas kernels for 0%

profile of v1, /device:TPU:0, one launch (start us, length us, event | category | flops | bytes accessed | tf_op | source)
XLA Modules:
  0.0 1459.1 jit_solution(3446551039515062742)
XLA Ops:
  14.4 2.9 collective-permute-start.3
  18.2 29.5 %collective-permute-done.3 = bf16[96,6144]{1,0:T(8,128)(2,1)} collective-permute-done((bf16[96,6144]{1,0:T(8,128)(2,1)S(1)}, bf16[96,6144]{1,0:T(8,128)(2,1)}, u32[]{:S(2)}, u32[]{:S(2)}) %collective-permute-start.3) | collective-permute-done | bytes 1179680 | tf_op jit(solution)/shard_map/ppermute | solution.py:24
  47.7 2.1 maximum_select_fusion.2
  51.7 72.6 %collective-permute-done.4 = bf16[192,6144]{1,0:T(8,128)(2,1)} collective-permute-done((bf16[192,6144]{1,0:T(8,128)(2,1)S(1)}, bf16[192,6144]{1,0:T(8,128)(2,1)}, u32[]{:S(2)}, u32[]{:S(2)}) %collective-permute-start.4) | collective-permute-done | bytes 2359328 | tf_op jit(solution)/shard_map/ppermute | solution.py:24
  124.3 6.4 maximum_select_fusion.1
  130.7 2.3 collective-permute-start.5
  134.3 120.8 %all-gather.2 = bf16[1,2,768]{1,0,2:T(2,128)(2,1)S(1)} all-gather(bf16[1,2,48]{1,0,2:T(2,128)(2,1)S(1)} %copy.83), channel_id=4, replica_groups=mesh['section'=2,'dp'=16] {'dp'}, dimensions={2}, use_global_device_ids=true | all-gather | bytes 3264 | tf_op jit(solution)/shard_map/all_gather | solution.py:228
  255.9 142.9 %all-gather.3 = bf16[1,2,768]{1,0,2:T(2,128)(2,1)S(1)} all-gather(bf16[1,2,48]{1,0,2:T(2,128)(2,1)S(1)} %copy.85), channel_id=5, replica_groups=mesh['section'=2,'dp'=16] {'dp'}, dimensions={2}, use_global_device_ids=true | all-gather | bytes 3264 | tf_op jit(solution)/shard_map/all_gather | solution.py:229
  399.7 12.1 maximum_select_fusion
  423.4 6.1 broadcast_in_dim.183
  429.6 169.1 %while.65 = (s32[]{:T(128)}, bf16[256,768]{1,0:T(8,128)(2,1)}, bf16[2,256,768]{2,1,0:T(8,128)(2,1)}, bf16[2,256,768]{2,1,0:T(8,128)(2,1)}, bf16[2,256,1536]{2,1,...) while((s32[]{:T(128)}, bf16[256,768]{1,0:T(8,128)(2,1)}, ...), condition=%wide.region_7.8_spmd, body=%wide.region_0.7_spmd.sunk | while | flops 5104144384 | bytes 180324528 | solution.py:274
  440.7 3.2 convolution_convert_fusion.4
  449.4 4.3 constant_dynamic-slice_fusion.29
  453.8 6.1 bitcast_dynamic-update-slice_fusion.15
  460.0 11.2 fusion.202
  472.6 4.2 collective-permute-start
  483.8 2.6 bitcast_dynamic-update-slice_fusion.18
  497.5 3.1 convolution_convert_fusion.4
  506.1 4.1 constant_dynamic-slice_fusion.29
  510.3 6.3 bitcast_dynamic-update-slice_fusion.15
  516.6 11.2 fusion.202
  529.2 4.0 collective-permute-start
  540.2 2.6 bitcast_dynamic-update-slice_fusion.18
  553.9 3.1 convolution_convert_fusion.4
  562.5 4.1 constant_dynamic-slice_fusion.29
  566.7 6.3 bitcast_dynamic-update-slice_fusion.15
  573.0 11.2 fusion.202
  585.7 3.4 collective-permute-start
  596.0 2.6 bitcast_dynamic-update-slice_fusion.18
  601.2 258.6 %while.66 = (s32[]{:T(128)}, bf16[256,768]{1,0:T(8,128)(2,1)}, f32[768,2304]{1,0:T(8,128)}, f32[768,768]{1,0:T(8,128)}, f32[768,6144]{1,0:T(8,128)}, /*index=5*/...) while((s32[]{:T(128)}, bf16[256,768]{1,0:T(8,128)(2,1)}, ...), condition=%wide.region_18.19_spmd.clone, body=%wide.region_8.18_spmd.clone.sunk | while | flops 10294599680 | bytes 311429440 | solution.py:318
  610.6 2.3 fusion.225
  618.2 4.1 dynamic-slice_bitcast_fusion.4
  624.0 10.6 multiply_convert_fusion.8
  634.7 8.7 fusion.227
  650.6 2.1 fusion.234
  656.7 7.2 select_add_fusion.11
  663.9 5.1 select_add_fusion.8
  669.1 8.4 select_add_fusion.10
  677.5 2.9 select_add_fusion.9
  689.8 2.3 fusion.225
  697.5 4.1 dynamic-slice_bitcast_fusion.4
  703.3 10.6 multiply_convert_fusion.8
  714.0 8.7 fusion.227
  729.9 2.1 fusion.234
  734.9 2.1 bitcast_dynamic-update-slice_fusion.19
  737.0 10.0 select_add_fusion.11
  747.0 7.3 select_add_fusion.8
  754.3 12.0 select_add_fusion.10
  766.4 3.7 select_add_fusion.9
  779.5 2.3 fusion.225
  787.2 4.1 dynamic-slice_bitcast_fusion.4
  793.0 10.6 multiply_convert_fusion.8
  803.7 8.7 fusion.227
  819.6 2.1 fusion.234
  826.8 10.0 select_add_fusion.11
  836.7 7.3 select_add_fusion.8
  844.0 12.0 select_add_fusion.10
  856.1 3.7 select_add_fusion.9
  866.0 52.1 %reduce-scatter.21.cloned.1.call-done = f32[48,2]{1,0:T(8,128)} async-done(((f32[768,2]{1,0:T(8,128)}), f32[48,2]{1,0:T(8,128)}) %reduce-scatter.21.cloned.1.call-update) | async-done | bytes 400
  919.5 57.0 %reduce-scatter.19.cloned.1.call-done = f32[48,2]{1,0:T(8,128)} async-done(((f32[768,2]{1,0:T(8,128)}), f32[48,2]{1,0:T(8,128)}) %reduce-scatter.19.cloned.1.call-update) | async-done | bytes 400
  977.9 65.0 %reduce-scatter.13.cloned.1.call-done = f32[48,768]{1,0:T(8,128)} async-done(((f32[768,768]{1,0:T(8,128)}), f32[48,768]{1,0:T(8,128)}) %reduce-scatter.13.cloned.1.call-update) | async-done | bytes 147472 | tf_op jit(solution)/shard_map/reduce_scatter | solution.py:323
  1042.8 94.2 %reduce-scatter.11.cloned.1.call-done = f32[48,2304]{1,0:T(8,128)} async-done(((f32[768,2304]{1,0:T(8,128)}), f32[48,2304]{1,0:T(8,128)}) %reduce-scatter.11.cloned.1.call-update) | async-done | bytes 442384 | tf_op jit(solution)/shard_map/reduce_scatter | solution.py:322
  1137.0 115.6 %reduce-scatter.17.cloned.1.call-done = f32[192,768]{1,0:T(8,128)} async-done(((f32[3072,768]{1,0:T(8,128)}), f32[192,768]{1,0:T(8,128)}) %reduce-scatter.17.cloned.1.call-update) | async-done | bytes 589840 | tf_op jit(solution)/shard_map/reduce_scatter | solution.py:328
  1252.6 199.6 %reduce-scatter.15.cloned.1.call-done = f32[48,6144]{1,0:T(8,128)} async-done(((f32[768,6144]{1,0:T(8,128)}), f32[48,6144]{1,0:T(8,128)}) %reduce-scatter.15.cloned.1.call-update) | async-done | bytes 1179664 | tf_op jit(solution)/shard_map/reduce_scatter | solution.py:327
  (654 shorter events, 188.1 us)
Async XLA Ops:
  7.2 10.2 copy-start.31
  7.2 404.6 %all-gather.13.cloned.1.call-start = ((), (), s32[]{:S(2)}) async-start(), calls=%async_computation.11 | async-start | bytes 1253376 | tf_op jit(solution)/shard_map/all_gather | solution.py:225
  8.9 402.9 %all-gather.11.cloned.1.call-start = ((), (), s32[]{:S(2)}) async-start(), calls=%async_computation.10 | async-start | bytes 3760128 | tf_op jit(solution)/shard_map/all_gather | solution.py:224
  10.7 401.1 %all-gather.15.cloned.1.call-start = ((), (), s32[]{:S(2)}) async-start(), calls=%async_computation.12 | async-start | bytes 5013504 | tf_op jit(solution)/shard_map/all_gather | solution.py:227
  12.0 2.1 collective-permute-start.2
  14.4 33.3 %collective-permute-start.3 = (bf16[96,6144]{1,0:T(8,128)(2,1)S(1)}, bf16[96,6144]{1,0:T(8,128)(2,1)}, u32[]{:S(2)}, u32[]{:S(2)}) collective-permute-start(bf16[96,6144]{1,0:T(8,128)(2,1)S(1)} %maximum_select_fusion.3), channel_id=1, source_target_pairs={{0,2},{1,3},{2,0},{3,1},{4,6},{5,7},{6,4},{7,5},{8,10},{9,11},{10,... | collective-permute-start | bytes 3538952 | tf_op jit(solution)/shard_map/ppermute | solution.py:24
  18.1 580.5 %all-gather.17.cloned.1.call-start = ((), (), s32[]{:S(2)}) async-start(), calls=%async_computation.13 | async-start | bytes 10027008 | tf_op jit(solution)/shard_map/all_gather | solution.py:278
  49.8 74.5 %collective-permute-start.4 = (bf16[192,6144]{1,0:T(8,128)(2,1)S(1)}, bf16[192,6144]{1,0:T(8,128)(2,1)}, u32[]{:S(2)}, u32[]{:S(2)}) collective-permute-start(bf16[192,6144]{1,0:T(8,128)(2,1)S(1)} %maximum_select_fusion.2), channel_id=1, source_target_pairs={{0,4},{1,5},{2,6},{3,7},{4,0},{5,1},{6,2},{7,3},{8,12},{9,13},{10,... | collective-permute-start | bytes 7077896 | tf_op jit(solution)/shard_map/ppermute | solution.py:24
  51.7 81.3 %copy-start.26 = (f32[1,48,6144]{2,1,0:T(8,128)S(1)}, f32[1,48,6144]{2,1,0:T(8,128)}, u32[]{:S(2)}) copy-start(f32[1,48,6144]{2,1,0:T(8,128)} %param.17) | copy-start | bytes 3538948
  51.7 82.3 %copy-start.56 = (f32[1,2,48]{2,1,0:T(2,128)S(1)}, f32[1,2,48]{2,1,0:T(2,128)}, u32[]{:S(2)}) copy-start(f32[1,2,48]{2,1,0:T(2,128)} %param.19) | copy-start | bytes 1156
  51.7 82.3 %copy-start.57 = (f32[1,2,48]{2,1,0:T(2,128)S(1)}, f32[1,2,48]{2,1,0:T(2,128)}, u32[]{:S(2)}) copy-start(f32[1,2,48]{2,1,0:T(2,128)} %param.20) | copy-start | bytes 1156
  130.7 269.0 %collective-permute-start.5 = (bf16[384,6144]{1,0:T(8,128)(2,1)}, bf16[384,6144]{1,0:T(8,128)(2,1)}, u32[]{:S(2)}, u32[]{:S(2)}) collective-permute-start(bf16[384,6144]{1,0:T(8,128)(2,1)} %maximum_select_fusion.1), channel_id=1, source_target_pairs={{0,8},{1,9},{2,10},{3,11},{4,12},{5,13},{6,14},{7,15},{8,0},{9,1},... | collective-permute-start | bytes 14155784 | tf_op jit(solution)/shard_map/ppermute | solution.py:24
  133.9 784.2 %reduce-scatter.21.cloned.1.call-start = ((), (), s32[]{:S(2)}) async-start(), calls=%async_computation.15 | async-start | bytes 417792
  460.0 11.5 copy-start.35
  460.0 11.5 copy-start.36
  460.0 16.8 %copy-start.22 = (bf16[2,256,768]{2,1,0:T(8,128)(2,1)S(1)}, bf16[2,256,768]{2,1,0:T(8,128)(2,1)}, u32[]{:S(2)}) copy-start(bf16[2,256,768]{2,1,0:T(8,128)(2,1)} %get-tuple-element.1917) | copy-start | bytes 2359300 | tf_op jit(solution)/shard_map/while
  460.0 16.9 %copy-start.19 = (bf16[2,256,768]{2,1,0:T(8,128)(2,1)S(1)}, bf16[2,256,768]{2,1,0:T(8,128)(2,1)}, u32[]{:S(2)}) copy-start(bf16[2,256,768]{2,1,0:T(8,128)(2,1)} %get-tuple-element.1923) | copy-start | bytes 2359300 | tf_op jit(solution)/shard_map/while
  471.4 10.2 copy-start.38
  472.6 13.7 collective-permute-start
  516.6 11.5 copy-start.35
  516.6 11.5 copy-start.36
  516.6 16.7 %copy-start.22 = (bf16[2,256,768]{2,1,0:T(8,128)(2,1)S(1)}, bf16[2,256,768]{2,1,0:T(8,128)(2,1)}, u32[]{:S(2)}) copy-start(bf16[2,256,768]{2,1,0:T(8,128)(2,1)} %get-tuple-element.1917) | copy-start | bytes 2359300 | tf_op jit(solution)/shard_map/while
  516.6 16.7 %copy-start.19 = (bf16[2,256,768]{2,1,0:T(8,128)(2,1)S(1)}, bf16[2,256,768]{2,1,0:T(8,128)(2,1)}, u32[]{:S(2)}) copy-start(bf16[2,256,768]{2,1,0:T(8,128)(2,1)} %get-tuple-element.1923) | copy-start | bytes 2359300 | tf_op jit(solution)/shard_map/while
  528.1 10.0 copy-start.38
  529.2 13.6 collective-permute-start
  573.0 11.5 copy-start.35
  573.0 11.5 copy-start.36
  573.0 16.0 %copy-start.22 = (bf16[2,256,768]{2,1,0:T(8,128)(2,1)S(1)}, bf16[2,256,768]{2,1,0:T(8,128)(2,1)}, u32[]{:S(2)}) copy-start(bf16[2,256,768]{2,1,0:T(8,128)(2,1)} %get-tuple-element.1917) | copy-start | bytes 2359300 | tf_op jit(solution)/shard_map/while
  573.0 16.1 %copy-start.19 = (bf16[2,256,768]{2,1,0:T(8,128)(2,1)S(1)}, bf16[2,256,768]{2,1,0:T(8,128)(2,1)}, u32[]{:S(2)}) copy-start(bf16[2,256,768]{2,1,0:T(8,128)(2,1)} %get-tuple-element.1923) | copy-start | bytes 2359300 | tf_op jit(solution)/shard_map/while
  584.5 9.4 copy-start.38
  585.7 12.9 collective-permute-start
  622.4 12.3 copy-start
  624.0 10.7 copy-start.6
  624.0 10.7 copy-start.12
  624.0 10.7 copy-start.37
  634.7 8.7 copy-start.13
  634.7 8.7 copy-start.15
  652.8 27.6 %collective-permute-start.1 = (bf16[256,768]{1,0:T(8,128)(2,1)}, bf16[256,768]{1,0:T(8,128)(2,1)}, u32[]{:S(2)}, u32[]{:S(2)}) collective-permute-start(bf16[256,768]{1,0:T(8,128)(2,1)} %get-tuple-element.1876), channel_id=1, source_target_pairs={{16,0},{17,1},{18,2},{19,3},{20,4},{21,5},{22,6},{23,7},{24,8},{25... | collective-permute-start | bytes 1179656 | tf_op jit(solution)/shard_map/while/body/eval_jaxpr/ppermute | solution.py:38
  701.6 12.3 copy-start
  703.2 10.7 copy-start.6
  703.3 10.7 copy-start.12
  703.3 10.7 copy-start.37
  713.9 8.7 copy-start.13
  713.9 8.7 copy-start.15
  732.0 38.0 %collective-permute-start.1 = (bf16[256,768]{1,0:T(8,128)(2,1)}, bf16[256,768]{1,0:T(8,128)(2,1)}, u32[]{:S(2)}, u32[]{:S(2)}) collective-permute-start(bf16[256,768]{1,0:T(8,128)(2,1)} %get-tuple-element.1876), channel_id=1, source_target_pairs={{16,0},{17,1},{18,2},{19,3},{20,4},{21,5},{22,6},{23,7},{24,8},{25... | collective-permute-start | bytes 1179656 | tf_op jit(solution)/shard_map/while/body/eval_jaxpr/ppermute | solution.py:38
  737.0 10.0 copy-start.18
  754.3 12.0 copy-start.39
  754.3 12.0 copy-start.41
  791.3 12.3 copy-start
  792.9 10.7 copy-start.6
  793.0 10.7 copy-start.12
  793.0 10.7 copy-start.37
  803.6 8.7 copy-start.13
  803.6 8.7 copy-start.15
  803.7 8.7 copy-start.43
  821.7 38.1 %collective-permute-start.1 = (bf16[256,768]{1,0:T(8,128)(2,1)}, bf16[256,768]{1,0:T(8,128)(2,1)}, u32[]{:S(2)}, u32[]{:S(2)}) collective-permute-start(bf16[256,768]{1,0:T(8,128)(2,1)} %get-tuple-element.1876), channel_id=1, source_target_pairs={{16,0},{17,1},{18,2},{19,3},{20,4},{21,5},{22,6},{23,7},{24,8},{25... | collective-permute-start | bytes 1179656 | tf_op jit(solution)/shard_map/while/body/eval_jaxpr/ppermute | solution.py:38
  826.8 10.0 copy-start.18
  844.0 12.0 copy-start.39
  844.0 12.0 copy-start.41
  861.5 115.0 %reduce-scatter.19.cloned.1.call-start = ((), (), s32[]{:S(2)}) async-start(), calls=%async_computation.14 | async-start | bytes 417792
  863.2 179.7 %reduce-scatter.13.cloned.1.call-start = ((), (), s32[]{:S(2)}) async-start(), calls=%async_computation.7 | async-start | bytes 2506752 | tf_op jit(solution)/shard_map/reduce_scatter | solution.py:323
  863.9 273.1 %reduce-scatter.11.cloned.1.call-start = ((), (), s32[]{:S(2)}) async-start(), calls=%async_computation.6 | async-start | bytes 7520256 | tf_op jit(solution)/shard_map/reduce_scatter | solution.py:322
  864.7 387.9 %reduce-scatter.17.cloned.1.call-start = ((), (), s32[]{:S(2)}) async-start(), calls=%async_computation.9 | async-start | bytes 10027008 | tf_op jit(solution)/shard_map/reduce_scatter | solution.py:328
  865.4 586.8 %reduce-scatter.15.cloned.1.call-start = ((), (), s32[]{:S(2)}) async-start(), calls=%async_computation.8 | async-start | bytes 20054016 | tf_op jit(solution)/shard_map/reduce_scatter | solution.py:327
  (135 other events, 536.5 us)
Sparse Core Ops, SparseCore 0:
  10.9 43.8 all-gather.12
  57.6 58.2 all-gather.10
  118.7 169.3 all-gather.14
  290.8 160.7 all-gather.16
  861.6 56.4 reduce-scatter.20
  921.9 54.5 reduce-scatter.18
  980.8 61.9 reduce-scatter.12
  1048.0 89.0 reduce-scatter.10
  1141.7 110.8 reduce-scatter.16
  1257.7 194.5 reduce-scatter.14
